TPU v7x, 32 devices: a whole 2x2x4 slice. The times are simulated.
32 devices in a mesh: img: 8 (over y, x, core), seq: 4 (over z).
Axes of the slice: x: 2, y: 2, z: 4, core: 2. Of those that a mesh axis runs over, the one named last changes fastest.
Arguments:
- x_big: bfloat16 [128, 200, 768], P(('img', 'seq')), may hold values from -6 to 6
- x_small: bfloat16 [512, 40, 768], P(('img', 'seq')), may hold values from -6 to 6
- mask_big: int32 [128, 200], P('img'), may hold values from 0 to 1, as said below
- mask_small: int32 [512, 40], P('img'), may hold values from 0 to 1, as said below
- ln1_gain: float32 [768], P('seq'), may hold values from 0.5 to 1.5
- ln1_bias: float32 [768], P('seq'), may hold values from -1.75 to 1.75
- w_qkv: float32 [768, 2304], P('img', 'seq'), may hold values from -0.21875 to 0.21875
- b_qv: float32 [1536], P('seq'), may hold values from -3 to 3
- w_out: float32 [768, 768], P('img', 'seq'), may hold values from -0.625 to 0.625
- b_out: float32 [768], P('seq'), may hold values from -1.75 to 1.75
- ln2_gain: float32 [768], P('seq'), may hold values from 0.5 to 1.5
- ln2_bias: float32 [768], P('seq'), may hold values from -1.75 to 1.75
- w_up: float32 [768, 3072], P('img', 'seq'), may hold values from -0.21875 to 0.21875
- b_up: float32 [3072], P('seq'), may hold values from -3 to 3
- w_down: float32 [3072, 768], P('img', 'seq'), may hold values from -0.109375 to 0.109375
- b_down: float32 [768], P('seq'), may hold values from -1.75 to 1.75
- dy_big: bfloat16 [128, 200, 768], P(('img', 'seq')), may hold values from -6 to 6
- dy_small: bfloat16 [512, 40, 768], P(('img', 'seq')), may hold values from -6 to 6
Outputs:
- y_big: bfloat16 [128, 200, 768], P(('img', 'seq'))
- y_small: bfloat16 [512, 40, 768], P(('img', 'seq'))
- dx_big: bfloat16 [128, 200, 768], P(('img', 'seq'))
- dx_small: bfloat16 [512, 40, 768], P(('img', 'seq'))
- g_ln1_gain: float32 [768], P('seq')
- g_ln1_bias: float32 [768], P('seq')
- g_w_qkv: float32 [768, 2304], P('img', 'seq')
- g_b_qv: float32 [1536], P('seq')
- g_w_out: float32 [768, 768], P('img', 'seq')
- g_b_out: float32 [768], P('seq')
- g_ln2_gain: float32 [768], P('seq')
- g_ln2_bias: float32 [768], P('seq')
- g_w_up: float32 [768, 3072], P('img', 'seq')
- g_b_up: float32 [3072], P('seq')
- g_w_down: float32 [3072, 768], P('img', 'seq')
- g_b_down: float32 [768], P('seq')
Inputs may be any that keep to these rules, and one draw needn't show every extreme that they name: `mask_big`: each 224px crop's mask is 1 on its first 175 to 200 slots and 0 after; some crop has all slots valid and some the fewest. `mask_small`: each 96px crop's mask is 1 on its first 35 to 40 slots and 0 after; some crop has all slots valid and some the fewest.
All inputs are finite; a program needn't handle non-finite values.
Results may differ from a plain program's by a relative error of at most 0.014.
Values may be sent and summed in bfloat16 or wider, within the bound.
A program may use at most 192 MiB of HBM per device.

v0:
```python
import jax
import jax.numpy as jnp
from jax import lax
from jax.sharding import PartitionSpec as P

HEADS = 12
HEAD_DIM = 64
AXES = ("img", "seq")
EPSILON = 1e-06
NEGATIVE = -1e30


def layer_norm(values, gain_vec, shift_vec):
    row_mean = jnp.mean(values, axis=-1, keepdims=True)
    centred = values - row_mean
    variance = jnp.mean(centred * centred, axis=-1, keepdims=True)
    return centred * lax.rsqrt(variance + EPSILON) * gain_vec + shift_vec


def gelu_exact(values):
    return jax.nn.gelu(values, approximate=False)


def head_scores(heads_in, key_valid):
    crop_count, length = (heads_in.shape[0], heads_in.shape[1])
    pieces = heads_in.reshape(crop_count, length, 3, HEADS, HEAD_DIM)
    queries, key_rows, value_rows = (pieces[:, :, 0], pieces[:, :, 1], pieces[:, :, 2])
    raw_scores = jnp.einsum(
        "cqhd,ckhd->chqk", queries, key_rows, preferred_element_type=jnp.float32
    )
    scores = jnp.where(key_valid[:, None, None, :] > 0, raw_scores * HEAD_DIM ** (-0.5), NEGATIVE)
    return (queries, key_rows, value_rows, scores)


def attend(heads_in, key_valid):
    crop_count, length = (heads_in.shape[0], heads_in.shape[1])
    queries, key_rows, value_rows, scores = head_scores(heads_in, key_valid)
    row_max = jnp.max(scores, axis=-1, keepdims=True)
    exponent = jnp.exp(scores - row_max)
    row_total = jnp.sum(exponent, axis=-1, keepdims=True)
    softmax_w = (exponent / row_total).astype(jnp.bfloat16)
    mixed_out = jnp.einsum(
        "chqk,ckhd->cqhd", softmax_w, value_rows, preferred_element_type=jnp.float32
    )
    log_total = row_max + jnp.log(row_total)
    return (mixed_out.astype(jnp.bfloat16).reshape(crop_count * length, -1), log_total)


def attend_back(heads_in, key_valid, log_total, grad_heads):
    crop_count, length = (heads_in.shape[0], heads_in.shape[1])
    queries, key_rows, value_rows, scores = head_scores(heads_in, key_valid)
    softmax_f = jnp.exp(scores - log_total)
    grad_mixed = grad_heads.reshape(crop_count, length, HEADS, HEAD_DIM)
    grad_soft = jnp.einsum(
        "cqhd,ckhd->chqk", grad_mixed, value_rows, preferred_element_type=jnp.float32
    )
    inner_sum = jnp.sum(softmax_f * grad_soft, axis=-1, keepdims=True)
    grad_raw = (softmax_f * (grad_soft - inner_sum) * HEAD_DIM ** (-0.5)).astype(jnp.bfloat16)
    grad_query = jnp.einsum(
        "chqk,ckhd->cqhd", grad_raw, key_rows, preferred_element_type=jnp.float32
    )
    grad_key = jnp.einsum("chqk,cqhd->ckhd", grad_raw, queries, preferred_element_type=jnp.float32)
    grad_value = jnp.einsum(
        "chqk,cqhd->ckhd",
        softmax_f.astype(jnp.bfloat16),
        grad_mixed,
        preferred_element_type=jnp.float32,
    )
    stacked = jnp.stack([grad_query, grad_key, grad_value], axis=2).astype(jnp.bfloat16)
    return stacked.reshape(crop_count * length, -1)


def gather_mats(mats):
    n_img, n_seq = (lax.axis_size("img"), lax.axis_size("seq"))
    flat = jnp.concatenate([m.astype(jnp.bfloat16).reshape(-1, 64) for m in mats], axis=0)
    whole = lax.all_gather(flat, AXES, axis=0, tiled=False)
    outs, at = ([], 0)
    for m in mats:
        rows = m.size // 64
        piece = whole[:, at : at + rows].reshape((n_img, n_seq) + m.shape)
        at += rows
        if m.ndim == 2:
            piece = piece.transpose(0, 2, 1, 3).reshape(n_img * m.shape[0], n_seq * m.shape[1])
        else:
            piece = piece[0].reshape(-1)
        outs.append(piece)
    return outs


def scatter_mats(mats):
    n_img, n_seq = (lax.axis_size("img"), lax.axis_size("seq"))
    blocks = []
    for m in mats:
        rows, cols = (m.shape[0] // n_img, m.shape[1] // n_seq)
        b = m.astype(jnp.bfloat16).reshape(n_img, rows, n_seq, cols).transpose(0, 2, 1, 3)
        blocks.append(b.reshape(n_img * n_seq, -1, 128))
    flat = jnp.concatenate(blocks, axis=1)
    mine = lax.psum_scatter(flat, AXES, scatter_dimension=0, tiled=False)
    outs, at = ([], 0)
    for m, b in zip(mats, blocks):
        piece = mine[at : at + b.shape[1]]
        at += b.shape[1]
        outs.append(piece.reshape(m.shape[0] // n_img, m.shape[1] // n_seq).astype(jnp.float32))
    return outs


def body(
    x_big,
    x_small,
    mask_big,
    mask_small,
    ln1_gain,
    ln1_bias,
    w_qkv,
    b_qv,
    w_out,
    b_out,
    ln2_gain,
    ln2_bias,
    w_up,
    b_up,
    w_down,
    b_down,
    dy_big,
    dy_small,
):
    n_seq = lax.axis_size("seq")
    where = lax.axis_index("seq")
    model_width = x_big.shape[2]
    big_crops, big_length = (x_big.shape[0], x_big.shape[1])
    small_crops, small_length = (x_small.shape[0], x_small.shape[1])
    big_rows = big_crops * big_length
    mask_big = lax.dynamic_slice_in_dim(mask_big, where * big_crops, big_crops, 0)
    mask_small = lax.dynamic_slice_in_dim(mask_small, where * small_crops, small_crops, 0)
    qkv_full, gain_one, shift_one, bias_qv, bias_out, gain_two, shift_two, bias_up, bias_down = (
        gather_mats([w_qkv, ln1_gain, ln1_bias, b_qv, b_out, ln2_gain, ln2_bias, b_up, b_down])
    )
    out_full, up_full, down_full = gather_mats([w_out, w_up, w_down])
    gain_one, shift_one, bias_qv, bias_out, gain_two, shift_two, bias_up, bias_down = tuple(
        (
            vec.astype(jnp.float32)
            for vec in (
                gain_one,
                shift_one,
                bias_qv,
                bias_out,
                gain_two,
                shift_two,
                bias_up,
                bias_down,
            )
        )
    )
    tokens = jnp.concatenate(
        [x_big.reshape(big_rows, model_width), x_small.reshape(-1, model_width)], axis=0
    ).astype(jnp.float32)
    normed_one, pull_one = jax.vjp(layer_norm, tokens, gain_one, shift_one)
    input_one = normed_one.astype(jnp.bfloat16)
    bias_qkv = jnp.concatenate(
        [bias_qv[:model_width], jnp.zeros((model_width,), jnp.float32), bias_qv[model_width:]]
    )
    projected = (
        jnp.dot(input_one, qkv_full, preferred_element_type=jnp.float32) + bias_qkv
    ).astype(jnp.bfloat16)
    heads_big = projected[:big_rows].reshape(big_crops, big_length, -1)
    heads_small = projected[big_rows:].reshape(small_crops, small_length, -1)
    mixed_big, total_big = attend(heads_big, mask_big)
    mixed_small, total_small = attend(heads_small, mask_small)
    mixed_tok = jnp.concatenate([mixed_big, mixed_small], axis=0)
    middle = tokens + jnp.dot(mixed_tok, out_full, preferred_element_type=jnp.float32) + bias_out
    normed_two, pull_two = jax.vjp(layer_norm, middle, gain_two, shift_two)
    input_two = normed_two.astype(jnp.bfloat16)
    up_proj = jnp.dot(input_two, up_full, preferred_element_type=jnp.float32) + bias_up
    activated_f, pull_act = jax.vjp(gelu_exact, up_proj)
    activated = activated_f.astype(jnp.bfloat16)
    result = middle + jnp.dot(activated, down_full, preferred_element_type=jnp.float32) + bias_down
    grad_out = jnp.concatenate(
        [dy_big.reshape(big_rows, model_width), dy_small.reshape(-1, model_width)], axis=0
    )
    grad_down = jnp.einsum("ti,tj->ij", activated, grad_out, preferred_element_type=jnp.float32)
    grad_bias_down = jnp.sum(grad_out.astype(jnp.float32), axis=0)
    grad_act = jnp.einsum("tj,ij->ti", grad_out, down_full, preferred_element_type=jnp.float32)
    (grad_up_f,) = pull_act(grad_act)
    grad_up_b = grad_up_f.astype(jnp.bfloat16)
    grad_upw = jnp.einsum("ti,tj->ij", input_two, grad_up_b, preferred_element_type=jnp.float32)
    grad_bias_up = jnp.sum(grad_up_b.astype(jnp.float32), axis=0)
    grad_in_two = jnp.einsum("tj,ij->ti", grad_up_b, up_full, preferred_element_type=jnp.float32)
    grad_middle_ln, grad_gain_two, grad_shift_two = pull_two(grad_in_two)
    grad_middle = grad_out.astype(jnp.float32) + grad_middle_ln
    grad_branch = grad_middle.astype(jnp.bfloat16)
    grad_bias_out = jnp.sum(grad_branch.astype(jnp.float32), axis=0)
    grad_outw = jnp.einsum("ti,tj->ij", mixed_tok, grad_branch, preferred_element_type=jnp.float32)
    grad_mixed = jnp.einsum(
        "tj,ij->ti", grad_branch, out_full, preferred_element_type=jnp.float32
    ).astype(jnp.bfloat16)
    grad_projected = jnp.concatenate(
        [
            attend_back(heads_big, mask_big, total_big, grad_mixed[:big_rows]),
            attend_back(heads_small, mask_small, total_small, grad_mixed[big_rows:]),
        ],
        axis=0,
    )
    grad_qkvw = jnp.einsum(
        "ti,tj->ij", input_one, grad_projected, preferred_element_type=jnp.float32
    )
    grad_proj_sums = jnp.sum(grad_projected.astype(jnp.float32), axis=0)
    grad_bias_qv = jnp.concatenate(
        [grad_proj_sums[:model_width], grad_proj_sums[2 * model_width :]]
    )
    grad_in_one = jnp.einsum(
        "tj,ij->ti", grad_projected, qkv_full, preferred_element_type=jnp.float32
    )
    grad_tokens_ln, grad_gain_one, grad_shift_one = pull_one(grad_in_one)
    grad_tokens = (grad_middle + grad_tokens_ln).astype(jnp.bfloat16)
    vectors = (
        grad_gain_one,
        grad_shift_one,
        grad_bias_qv,
        grad_bias_out,
        grad_gain_two,
        grad_shift_two,
        grad_bias_up,
        grad_bias_down,
    )
    vector_sums = lax.psum(jnp.concatenate(vectors), AXES)
    vec_out, at = ([], 0)
    for v in vectors:
        width = v.shape[0] // n_seq
        vec_out.append(lax.dynamic_slice(vector_sums, (at + where * width,), (width,)))
        at += v.shape[0]
    g_up, g_down = scatter_mats([grad_upw, grad_down])
    g_qkv, g_out = scatter_mats([grad_qkvw, grad_outw])
    y_big = result[:big_rows].reshape(big_crops, big_length, model_width).astype(jnp.bfloat16)
    y_small = result[big_rows:].reshape(small_crops, small_length, model_width).astype(jnp.bfloat16)
    dx_big = grad_tokens[:big_rows].reshape(big_crops, big_length, model_width)
    dx_small = grad_tokens[big_rows:].reshape(small_crops, small_length, model_width)
    return (
        y_big,
        y_small,
        dx_big,
        dx_small,
        vec_out[0],
        vec_out[1],
        g_qkv,
        vec_out[2],
        g_out,
        vec_out[3],
        vec_out[4],
        vec_out[5],
        g_up,
        vec_out[6],
        g_down,
        vec_out[7],
    )


def solution(mesh):
    rows3 = P(AXES, None, None)
    placed = (
        rows3,
        rows3,
        P("img", None),
        P("img", None),
        P("seq"),
        P("seq"),
        P("img", "seq"),
        P("seq"),
        P("img", "seq"),
        P("seq"),
        P("seq"),
        P("seq"),
        P("img", "seq"),
        P("seq"),
        P("img", "seq"),
        P("seq"),
        rows3,
        rows3,
    )
    return jax.shard_map(
        body,
        mesh=mesh,
        in_specs=placed,
        out_specs=(rows3,) * 4
        + (
            P("seq"),
            P("seq"),
            P("img", "seq"),
            P("seq"),
            P("img", "seq"),
            P("seq"),
            P("seq"),
            P("seq"),
            P("img", "seq"),
            P("seq"),
            P("img", "seq"),
            P("seq"),
        ),
        check_vma=False,
    )
```

profile of v0, /device:TPU:0, one launch (start us, length us, event | category | flops | bytes accessed | tf_op | source)
XLA Modules:
  0.0 870.6 jit_solution(1051177203787296150)
XLA Ops:
  25.0 55.9 %all-gather.7.cloned.1.call-done = bf16[32,900,64]{1,2,0:T(8,128)(2,1)} async-done(((bf16[1,900,64]{1,2,0:T(8,128)(2,1)}), bf16[32,900,64]{1,2,0:T(8,128)(2,1)}) %all-gather.7.cloned.1.call-update) | async-done | bytes 3686416 | tf_op jit(solution)/shard_map/all_gather | solution.py:76
  97.2 10.8 %reshape.350 = bf16[8,4,96,576]{3,2,1,0:T(8,128)(2,1)} reshape(bf16[32,864,64]{2,1,0:T(8,128)(2,1)} %copy.143) | data formatting | bytes 7077888 | tf_op jit(solution)/shard_map/reshape | solution.py:80
  136.7 9.8 %reshape_reshape.9 = bf16[16,40,3,12,64]{4,3,2,1,0:T(8,128)(2,1)} reshape(bf16[640,2304]{1,0:T(8,128)(2,1)} %slice.190) | data formatting | bytes 5898240 | tf_op jit(solution)/shard_map/reshape;reshape | solution.py:26
  168.5 12.1 %reshape.398 = bf16[4,200,3,12,64]{4,3,2,1,0:T(8,128)(2,1)} reshape(bf16[800,2304]{1,0:T(8,128)(2,1)} %slice.186) | data formatting | bytes 7372800 | tf_op jit(solution)/shard_map/reshape;reshape | solution.py:26
  239.9 14.1 %fusion.135 = (bf16[32,1152,64]{1,2,0:T(8,128)(2,1)}, bf16[32,1152,64]{1,2,0:T(8,128)(2,1)}) fusion(bf16[32,2592,64]{1,2,0:T(8,128)(2,1)} %all-gather.9.cloned.1.call-done), kind=kLoop, calls=%fused_computation.187 | loop fusion | bytes 18874368 | tf_op jit(solution)/shard_map/slice | solution.py:80
  263.7 15.5 %reshape.361 = bf16[8,4,384,192]{3,2,1,0:T(8,128)(2,1)} reshape(bf16[32,1152,64]{2,1,0:T(8,128)(2,1)} %copy.174) | data formatting | bytes 9437184 | tf_op jit(solution)/shard_map/reshape | solution.py:80
  303.3 13.4 %reshape.359 = bf16[8,4,96,768]{3,2,1,0:T(8,128)(2,1)} reshape(bf16[32,1152,64]{2,1,0:T(8,128)(2,1)} %copy.170) | data formatting | bytes 9437184 | tf_op jit(solution)/shard_map/reshape | solution.py:80
  328.1 48.1 %multiply_convert_fusion = (bf16[1440,3072]{1,0:T(8,128)(2,1)}, f32[1440,3072]{1,0:T(8,128)}, f32[1440,3072]{1,0:T(8,128)}) fusion(f32[3072]{0:T(1024)S(1)} %reshape.382, bf16[768,3072]{1,0:T(8,128)(2,1)S(1)} %bitcast.185, f32[1440,768]{1,0:T(8,128)S(1)} %get-tuple-element.108, f32[768]{0:T(1024)S(1)} %reshape.381, f32[768]{0:T(1024)S(1)} %reshape.380, ...), kind=kOutput, calls=%fused_computation.6 | convolution fusion | flops 7092264960 | bytes 53409024 | tf_op jit(solution)/shard_map/dot_general | solution.py:173
  376.3 21.3 %convert_reduce_fusion = (f32[3072]{0:T(1024)}, bf16[1440,3072]{1,0:T(8,128)(2,1)}) fusion(f32[1440,3072]{1,0:T(8,128)} %get-tuple-element.76, bf16[3072,768]{0,1:T(8,128)(2,1)S(1)} %bitcast.184, bf16[640,768]{1,0:T(8,128)(2,1)} %bitcast.187, bf16[800,768]{1,0:T(8,128)(2,1)S(1)} %bitcast.177, f32[1440,3072]{1,0:T(8,128)} %get-tuple-element.109, ...), kind=kOutput, calls=%fused_computation.4 | convolution fusion | flops 6874395648 | bytes 51191808 | tf_op jit(solution)/shard_map/tj,ij->ti/dot_general | solution.py:182
  397.6 13.7 %multiply_reduce_fusion.1 = (f32[768]{0:T(1024)}, f32[1440]{0:T(1024)S(1)}, f32[768]{0:T(1024)}, f32[1440,768]{1,0:T(8,128)S(1)}) fusion(f32[1440,768]{1,0:T(8,128)S(1)} %get-tuple-element.108, f32[1440]{0:T(1024)S(1)} %fusion.104, f32[1440]{0:T(1024)S(1)} %broadcast_multiply_fusion, f32[768]{0:T(1024)S(1)} %reshape.380, ...), kind=kOutput, calls=%fused_computation.67 | convolution fusion | flops 6803616768 | bytes 22439808 | tf_op jit(solution)/shard_map/tj,ij->ti/dot_general | solution.py:187
  434.6 10.0 %convert_bitcast_fusion.2 = bf16[16,40,1,12,64]{4,1,3,0,2:T(8,128)(2,1)} fusion(f32[16,12,40,40]{2,3,1,0:T(8,128)} %fusion.100, f32[16,12,40,40]{2,3,1,0:T(8,128)} %copy-done.8, f32[16,12,40]{2,1,0:T(8,128)S(1)} %copy-done.35, bf16[16,40,1,12,64]{4,3,2,1,0:T(8,128)(2,1)} %copy-done.26), kind=kOutput, calls=%fused_computation.98 | convolution fusion | flops 41971240 | bytes 4454400 | tf_op jit(solution)/shard_map/chqk,ckhd->cqhd/dot_general | solution.py:59
  475.5 19.7 %fusion.92 = bf16[4,200,1,12,64]{1,4,3,0,2:T(8,128)(2,1)} fusion(f32[4,12,200,200]{2,3,1,0:T(8,128)} %fusion.81, f32[4,12,200]{2,1,0:T(8,128)S(1)} %copy-done.46, f32[4,12,200,200]{2,3,1,0:T(8,128)} %copy-done.3, pred[4,200]{1,0:T(4,128)(4,1)S(1)} %copy-done.52, bf16[4,200,1,12,64]{1,4,3,0,2:T(8,128)(2,1)S(1)} %copy-done.17), kind=kOutput, calls=%fused_computation.122 | convolution fusion | flops 267504192 | bytes 17856800 | tf_op jit(solution)/shard_map/chqk,ckhd->cqhd/dot_general | solution.py:59
  495.2 19.0 %fusion.87 = bf16[4,200,1,12,64]{1,4,3,0,2:T(8,128)(2,1)} fusion(f32[4,12,200,200]{2,3,1,0:T(8,128)} %fusion.81, f32[4,12,200]{2,1,0:T(8,128)S(1)} %copy-done.46, f32[4,12,200,200]{2,3,1,0:T(8,128)} %copy-done.3, pred[4,200]{1,0:T(4,128)(4,1)S(1)} %copy-done.52, bf16[4,200,1,12,64]{1,4,3,0,2:T(8,128)(2,1)S(1)} %copy-done.15), kind=kOutput, calls=%fused_computation.121 | convolution fusion | flops 267504192 | bytes 17856800 | tf_op jit(solution)/shard_map/chqk,cqhd->ckhd/dot_general | solution.py:62
  528.6 12.8 %copy.203 = bf16[16,40,3,12,64]{1,0,4,3,2:T(8,128)(2,1)} copy(bf16[16,40,3,12,64]{4,1,3,0,2:T(8,128)(2,1)} %pad_maximum_fusion.2) | data formatting | bytes 5898240 | tf_op jit(solution)/shard_map/convert_element_type | solution.py:69
  541.3 14.1 %reshape.397 = bf16[640,2304]{0,1:T(8,128)(2,1)} reshape(bf16[16,40,3,12,64]{1,0,4,3,2:T(8,128)(2,1)} %copy.203) | data formatting | bytes 5898240 | tf_op jit(solution)/shard_map/convert_element_type | solution.py:69
  574.5 12.6 %convolution_convert_fusion = bf16[768,2304]{1,0:T(8,128)(2,1)} fusion(bf16[640,2304]{0,1:T(8,128)(2,1)} %reshape.397, bf16[800,2304]{0,1:T(8,128)(2,1)} %convert_element_type.280, f32[768]{0:T(1024)S(1)} %copy-done.54, f32[768]{0:T(1024)S(1)} %copy-done.48, f32[1440]{0:T(1024)S(1)} %copy-done.39, f32[1440]{0:T(1024)S(1)} %copy-done.37, ...), kind=kOutput, calls=%fused_computation.48 | convolution fusion | flops 5121073152 | bytes 12403968 | tf_op jit(solution)/shard_map/ti,tj->ij/dot_general | solution.py:203
  614.8 12.5 %convolution_convert_fusion.1 = bf16[3072,768]{1,0:T(8,128)(2,1)} fusion(bf16[1440,3072]{1,0:T(8,128)(2,1)} %get-tuple-element.75, bf16[640,768]{1,0:T(8,128)(2,1)} %bitcast.188, bf16[800,768]{1,0:T(8,128)(2,1)S(1)} %bitcast.179), kind=kOutput, calls=%fused_computation.49 | convolution fusion | flops 6801555456 | bytes 15777792 | tf_op jit(solution)/shard_map/ti,tj->ij/dot_general | solution.py:180
  639.7 14.1 %convolution_convert_fusion.2 = bf16[768,3072]{1,0:T(8,128)(2,1)} fusion(bf16[1440,3072]{1,0:T(8,128)(2,1)} %get-tuple-element.113, f32[1440,768]{1,0:T(8,128)} %copy-done.6, f32[768]{0:T(1024)S(1)} %copy-done.56, f32[768]{0:T(1024)S(1)} %reshape.380, f32[1440]{0:T(1024)S(1)} %fusion.104, f32[1440]{0:T(1024)S(1)} %broadcast_multiply_fusion), kind=kOutput, calls=%fused_computation.50 | convolution fusion | flops 6802661376 | bytes 18007296 | tf_op jit(solution)/shard_map/ti,tj->ij/dot_general | solution.py:185
  653.8 9.8 %reshape.373 = bf16[8,96,4,768]{3,2,1,0:T(4,128)(2,1)} reshape(bf16[768,3072]{1,0:T(8,128)(2,1)} %convolution_convert_fusion.2) | data formatting | bytes 9437184 | tf_op jit(solution)/shard_map/reshape | solution.py:95
  687.6 12.0 %reshape.376 = bf16[32,576,128]{2,1,0:T(8,128)(2,1)} reshape(bf16[8,4,384,192]{3,2,1,0:T(8,128)(2,1)} %copy.194) | data formatting | bytes 9437184 | tf_op jit(solution)/shard_map/reshape | solution.py:96
  708.4 13.1 %add_convert_fusion.2 = bf16[1440,768]{1,0:T(8,128)(2,1)S(1)} fusion(f32[1440,768]{1,0:T(8,128)} %copy-done.6, bf16[1440,3072]{1,0:T(8,128)(2,1)} %get-tuple-element.75, bf16[3072,768]{0,1:T(8,128)(2,1)} %bitcast.181, f32[768]{0:T(1024)S(1)} %reshape.383), kind=kOutput, calls=%fused_computation.71 | convolution fusion | flops 6798090240 | bytes 20204544 | tf_op jit(solution)/shard_map/dot_general | solution.py:176
  723.6 11.4 %fusion.131 = (f32[768]{0:T(1024)S(1)}, f32[1440]{0:T(1024)S(1)}, f32[1440,768]{1,0:T(8,128)S(1)}) fusion(f32[768]{0:T(1024)S(1)} %copy-done.48, f32[1440]{0:T(1024)S(1)} %copy-done.37, bf16[640,768]{1,0:T(8,128)(2,1)S(1)} %bitcast.172, bf16[800,768]{1,0:T(8,128)(2,1)S(1)} %bitcast.156, bf16[768,2304]{1,0:T(8,128)(2,1)} %reshape.351, ...), kind=kOutput, calls=%fused_computation.185 | convolution fusion | flops 5119301120 | bytes 16827648 | tf_op jit(solution)/shard_map/tj,ij->ti/dot_general | solution.py:210
  749.7 39.8 %psum.7 = f32[9216]{0:T(1024)S(1)} all-reduce(f32[9216]{0:T(1024)S(1)} %constant_dynamic-update-slice_fusion), channel_id=1, replica_groups=mesh['img'=8,'seq'=4] {'img','seq'}, use_global_device_ids=true, to_apply=%region_22.23 | all-reduce | flops 9216 | bytes 73728 | tf_op jit(solution)/shard_map/psum | solution.py:225
  794.7 66.3 %reduce-scatter.5.cloned.1.call-done = bf16[1,1152,128]{2,1,0:T(8,128)(2,1)} async-done(((bf16[32,1152,128]{2,1,0:T(8,128)(2,1)}), bf16[1,1152,128]{2,1,0:T(8,128)(2,1)}) %reduce-scatter.5.cloned.1.call-update) | async-done | bytes 294928 | tf_op jit(solution)/shard_map/reduce_scatter | solution.py:98
  (301 shorter events, 373.7 us)
Async XLA Ops:
  7.2 15.2 %copy-start = (s32[64,40]{0,1:T(8,128)S(1)}, s32[64,40]{0,1:T(8,128)}, u32[]{:S(2)}) copy-start(s32[64,40]{0,1:T(8,128)} %param.21) | copy-start | bytes 30724
  7.2 15.3 %copy-start.10 = (bf16[16,40,768]{2,1,0:T(8,128)(2,1)S(1)}, bf16[16,40,768]{2,1,0:T(8,128)(2,1)}, u32[]{:S(2)}) copy-start(bf16[16,40,768]{2,1,0:T(8,128)(2,1)} %param.19) | copy-start | bytes 2949124
  7.2 15.3 %copy-start.4 = (bf16[4,200,768]{2,1,0:T(8,128)(2,1)S(1)}, bf16[4,200,768]{2,1,0:T(8,128)(2,1)}, u32[]{:S(2)}) copy-start(bf16[4,200,768]{2,1,0:T(8,128)(2,1)} %param.18) | copy-start | bytes 3686404
  7.2 73.8 %all-gather.7.cloned.1.call-start = ((), (), s32[]{:S(2)}) async-start(), calls=%async_computation.4 | async-start | bytes 4325376 | tf_op jit(solution)/shard_map/all_gather | solution.py:76
  16.0 205.4 %all-gather.9.cloned.1.call-start = ((), (), s32[]{:S(2)}) async-start(), calls=%async_computation.5 | async-start | bytes 11354112 | tf_op jit(solution)/shard_map/all_gather | solution.py:76
  22.3 769.2 %reduce-scatter.3.cloned.1.call-start = ((), (), s32[]{:S(2)}) async-start(), calls=%async_computation.2 | async-start | bytes 4866048 | tf_op jit(solution)/shard_map/reduce_scatter | solution.py:98
  23.6 185.4 %copy-start.51 = (pred[4,200]{1,0:T(4,128)(4,1)}, pred[4,200]{1,0:T(4,128)(4,1)S(1)}, u32[]{:S(2)}) copy-start(pred[4,200]{1,0:T(4,128)(4,1)S(1)} %dynamic-slice_compare_fusion) | copy-start | bytes 2404
  23.6 98.3 %copy-start.36 = (f32[1440]{0:T(1024)}, f32[1440]{0:T(1024)S(1)}, u32[]{:S(2)}) copy-start(f32[1440]{0:T(1024)S(1)} %broadcast_multiply_fusion.1) | copy-start | bytes 17284
  25.0 96.9 %copy-start.38 = (f32[1440]{0:T(1024)}, f32[1440]{0:T(1024)S(1)}, u32[]{:S(2)}) copy-start(f32[1440]{0:T(1024)S(1)} %fusion.103) | copy-start | bytes 17284
  84.5 37.5 %copy-start.53 = (f32[768]{0:T(1024)}, f32[768]{0:T(1024)S(1)}, u32[]{:S(2)}) copy-start(f32[768]{0:T(1024)S(1)} %reshape.378) | copy-start | bytes 9220
  84.7 37.3 %copy-start.47 = (f32[768]{0:T(1024)}, f32[768]{0:T(1024)S(1)}, u32[]{:S(2)}) copy-start(f32[768]{0:T(1024)S(1)} %reshape.377) | copy-start | bytes 9220
  136.4 191.7 %copy-start.55 = (f32[768]{0:T(1024)}, f32[768]{0:T(1024)S(1)}, u32[]{:S(2)}) copy-start(f32[768]{0:T(1024)S(1)} %reshape.381) | copy-start | bytes 9220
  324.6 51.7 %slice-start.2 = ((s8[4718592]{0:T(1024)(128)(4,1)}), s8[524288]{0:T(1024)(128)(4,1)S(1)}, s32[]{:S(2)}) async-start(s8[4718592]{0:T(1024)(128)(4,1)} %bitcast.182), calls=%async_computation.8 | async-start | bytes 1048576
  327.4 83.9 %copy-start.6 = (f32[1440,768]{1,0:T(8,128)}, f32[1440,768]{1,0:T(8,128)S(1)}, u32[]{:S(2)}) copy-start(f32[1440,768]{1,0:T(8,128)S(1)} %get-tuple-element.108) | copy-start | bytes 13271044
  328.1 48.2 %copy-start.44 = (f32[1440]{0:T(1024)}, f32[1440]{0:T(1024)S(1)}, u32[]{:S(2)}) copy-start(f32[1440]{0:T(1024)S(1)} %multiply_reduce_fusion.3) | copy-start | bytes 17284
  328.1 48.2 %copy-start.19 = (bf16[4,200,768]{2,1,0:T(8,128)(2,1)S(1)}, bf16[4,200,768]{2,1,0:T(8,128)(2,1)}, u32[]{:S(2)}) copy-start(bf16[4,200,768]{2,1,0:T(8,128)(2,1)} %param.34) | copy-start | bytes 3686404
  328.1 48.2 %slice-start.3 = ((s8[4718592]{0:T(1024)(128)(4,1)}), s8[4194304]{0:T(1024)(128)(4,1)S(1)}, s32[]{:S(2)}) async-start(s8[4718592]{0:T(1024)(128)(4,1)} %bitcast.182), calls=%async_computation.9 | async-start | bytes 8388608
  475.5 19.7 %copy-start.15 = (bf16[4,200,1,12,64]{1,4,3,0,2:T(8,128)(2,1)S(1)}, bf16[4,200,1,12,64]{1,4,3,0,2:T(8,128)(2,1)}, u32[]{:S(2)}) copy-start(bf16[4,200,1,12,64]{1,4,3,0,2:T(8,128)(2,1)} %copy.213) | copy-start | bytes 3686404
  495.2 19.0 %copy-start.32 = (bf16[768,768]{1,0:T(8,128)(2,1)S(1)}, bf16[768,768]{1,0:T(8,128)(2,1)}, u32[]{:S(2)}) copy-start(bf16[768,768]{1,0:T(8,128)(2,1)} %convolution_convert_fusion.4) | copy-start | bytes 3538948
  613.6 247.5 %reduce-scatter.5.cloned.1.call-start = ((), (), s32[]{:S(2)}) async-start(), calls=%async_computation.3 | async-start | bytes 9732096 | tf_op jit(solution)/shard_map/reduce_scatter | solution.py:98
  708.4 15.2 %copy-start.7 = (bf16[800,2304]{0,1:T(8,128)(2,1)S(1)}, bf16[800,2304]{0,1:T(8,128)(2,1)}, u32[]{:S(2)}) copy-start(bf16[800,2304]{0,1:T(8,128)(2,1)} %convert_element_type.280) | copy-start | bytes 11059204
  722.5 16.6 %slice-start = ((s8[4423680]{0:T(1024)(128)(4,1)}), s8[4194304]{0:T(1024)(128)(4,1)S(1)}, s32[]{:S(2)}) async-start(s8[4423680]{0:T(1024)(128)(4,1)} %bitcast.148), calls=%async_computation.6 | async-start | bytes 8388608
  723.6 15.5 %slice-start.1 = ((s8[4423680]{0:T(1024)(128)(4,1)}), s8[229376]{0:T(1024)(128)(4,1)S(1)}, s32[]{:S(2)}) async-start(s8[4423680]{0:T(1024)(128)(4,1)} %bitcast.148), calls=%async_computation.7 | async-start | bytes 458752
  745.3 118.5 %copy-start.1 = (s32[64,40]{0,1:T(8,128)S(1)}, s32[64,40]{0,1:T(8,128)}, u32[]{:S(2)}) copy-start(s32[64,40]{0,1:T(8,128)} %param.21) | copy-start | bytes 30724
  (43 other events, 238.0 us)
Sparse Core Ops, SparseCore 0:
  16.2 64.7 all-gather.6
  84.4 87.4 all-gather.8
  613.7 105.7 reduce-scatter.2
  726.2 134.7 reduce-scatter.4
where the time goes:
time: 880 us; the launch traced here: 871 us
  local copies, waits for them, and re-layouts  376 us (43%)
  matrix products  256 us (29%)
  waiting for transfers between devices  122 us (14%)
  other arithmetic  62.1 us (7%)
  blocking collectives  39.8 us (5%)
  between operations  14.9 us (2%)
    reduce_scatter x2, waiting for transfers between devices, scatter_mats(): mine = lax.psum_scatter(flat, AXES, scatter_dimension=0, tiled=False)  66.3 us
    all_gather x2, waiting for transfers between devices, gather_mats(): whole = lax.all_gather(flat, AXES, axis=0, tiled=False)  55.9 us
    slice x7, local copies, waits for them, and re-layouts, gather_mats(): piece = whole[:, at:at + rows].reshape((n_img, n_seq) + m.shape)  52.6 us
    dot_general x1, matrix products, body(): jnp.dot(input_two, up_full, preferred_element_type=jnp.float32) + bias_up  48.1 us
    reshape x4, local copies, waits for them, and re-layouts, gather_mats(): piece = whole[:, at:at + rows].reshape((n_img, n_seq) + m.shape)  44.4 us
    psum x1, blocking collectives, body(): vector_sums = lax.psum(jnp.concatenate(vectors), AXES)  39.8 us
    unnamed x144, local copies, waits for them, and re-layouts  36.7 us
    convert_element_type x3, local copies, waits for them, and re-layouts, attend_back(): jnp.stack([grad_query, grad_key, grad_value], axis=2).astype(jnp.bfloat16)  36.6 us
  transfers between devices with their start and end apart: 4, of which 2 were waited for; matrix products, arithmetic and copies ran while one was open for 33% of the time, Pallas kernels for 0%

commit v1 on v0

--- a/solution.py
+++ b/solution.py
@@ -222,7 +222,7 @@
         grad_bias_up,
         grad_bias_down,
     )
-    vector_sums = lax.psum(jnp.concatenate(vectors), AXES)
+    vector_sums = lax.psum(lax.psum(jnp.concatenate(vectors), "seq"), "img")
     vec_out, at = ([], 0)
     for v in vectors:
         width = v.shape[0] // n_seq

time: 880 us -> 880 us (level)
    psum x1 -> x2, blocking collectives: 39.8 us -> 41.8 us  [body(): vector_sums = lax.psum(lax.psum(jnp.concatenate(vectors), 'seq'), 'img')]
where the time goes in v1:
time: 880 us; the launch traced here: 870 us
  local copies, waits for them, and re-layouts  376 us (43%)
  matrix products  255 us (29%)
  waiting for transfers between devices  120 us (14%)
  other arithmetic  62.1 us (7%)
  blocking collectives  41.8 us (5%)
  between operations  14.9 us (2%)
    reduce_scatter x2, waiting for transfers between devices, scatter_mats(): mine = lax.psum_scatter(flat, AXES, scatter_dimension=0, tiled=False)  64.2 us
    all_gather x2, waiting for transfers between devices, gather_mats(): whole = lax.all_gather(flat, AXES, axis=0, tiled=False)  55.9 us
    slice x7, local copies, waits for them, and re-layouts, gather_mats(): piece = whole[:, at:at + rows].reshape((n_img, n_seq) + m.shape)  52.5 us
    dot_general x1, matrix products, body(): jnp.dot(input_two, up_full, preferred_element_type=jnp.float32) + bias_up  48.1 us
    reshape x4, local copies, waits for them, and re-layouts, gather_mats(): piece = whole[:, at:at + rows].reshape((n_img, n_seq) + m.shape)  44.4 us
    psum x2, blocking collectives, body(): vector_sums = lax.psum(lax.psum(jnp.concatenate(vectors), 'seq'), 'img')  41.8 us
    unnamed x144, local copies, waits for them, and re-layouts  36.6 us
    convert_element_type x3, local copies, waits for them, and re-layouts, attend_back(): jnp.stack([grad_query, grad_key, grad_value], axis=2).astype(jnp.bfloat16)  36.6 us
  transfers between devices with their start and end apart: 4, of which 2 were waited for; matrix products, arithmetic and copies ran while one was open for 33% of the time, Pallas kernels for 0%

profile of v1, /device:TPU:0, one launch (start us, length us, event | category | flops | bytes accessed | tf_op | source)
XLA Modules:
  0.0 870.3 jit_solution(5268205859534864148)
XLA Ops:
  25.0 55.9 %all-gather.7.cloned.1.call-done = bf16[32,900,64]{1,2,0:T(8,128)(2,1)} async-done(((bf16[1,900,64]{1,2,0:T(8,128)(2,1)}), bf16[32,900,64]{1,2,0:T(8,128)(2,1)}) %all-gather.7.cloned.1.call-update) | async-done | bytes 3686416 | tf_op jit(solution)/shard_map/all_gather | solution.py:76
  97.2 10.8 %reshape.350 = bf16[8,4,96,576]{3,2,1,0:T(8,128)(2,1)} reshape(bf16[32,864,64]{2,1,0:T(8,128)(2,1)} %copy.143) | data formatting | bytes 7077888 | tf_op jit(solution)/shard_map/reshape | solution.py:80
  136.8 9.8 %reshape_reshape.9 = bf16[16,40,3,12,64]{4,3,2,1,0:T(8,128)(2,1)} reshape(bf16[640,2304]{1,0:T(8,128)(2,1)} %slice.190) | data formatting | bytes 5898240 | tf_op jit(solution)/shard_map/reshape;reshape | solution.py:26
  168.6 12.1 %reshape.398 = bf16[4,200,3,12,64]{4,3,2,1,0:T(8,128)(2,1)} reshape(bf16[800,2304]{1,0:T(8,128)(2,1)} %slice.186) | data formatting | bytes 7372800 | tf_op jit(solution)/shard_map/reshape;reshape | solution.py:26
  240.0 14.1 %fusion.135 = (bf16[32,1152,64]{1,2,0:T(8,128)(2,1)}, bf16[32,1152,64]{1,2,0:T(8,128)(2,1)}) fusion(bf16[32,2592,64]{1,2,0:T(8,128)(2,1)} %all-gather.9.cloned.1.call-done), kind=kLoop, calls=%fused_computation.187 | loop fusion | bytes 18874368 | tf_op jit(solution)/shard_map/slice | solution.py:80
  263.7 15.5 %reshape.361 = bf16[8,4,384,192]{3,2,1,0:T(8,128)(2,1)} reshape(bf16[32,1152,64]{2,1,0:T(8,128)(2,1)} %copy.174) | data formatting | bytes 9437184 | tf_op jit(solution)/shard_map/reshape | solution.py:80
  303.2 13.3 %reshape.359 = bf16[8,4,96,768]{3,2,1,0:T(8,128)(2,1)} reshape(bf16[32,1152,64]{2,1,0:T(8,128)(2,1)} %copy.170) | data formatting | bytes 9437184 | tf_op jit(solution)/shard_map/reshape | solution.py:80
  328.1 48.1 %multiply_convert_fusion = (bf16[1440,3072]{1,0:T(8,128)(2,1)}, f32[1440,3072]{1,0:T(8,128)}, f32[1440,3072]{1,0:T(8,128)}) fusion(f32[3072]{0:T(1024)S(1)} %reshape.382, bf16[768,3072]{1,0:T(8,128)(2,1)S(1)} %bitcast.185, f32[1440,768]{1,0:T(8,128)S(1)} %get-tuple-element.108, f32[768]{0:T(1024)S(1)} %reshape.381, f32[768]{0:T(1024)S(1)} %reshape.380, ...), kind=kOutput, calls=%fused_computation.6 | convolution fusion | flops 7092264960 | bytes 53409024 | tf_op jit(solution)/shard_map/dot_general | solution.py:173
  376.2 21.3 %convert_reduce_fusion = (f32[3072]{0:T(1024)}, bf16[1440,3072]{1,0:T(8,128)(2,1)}) fusion(f32[1440,3072]{1,0:T(8,128)} %get-tuple-element.76, bf16[3072,768]{0,1:T(8,128)(2,1)S(1)} %bitcast.184, bf16[640,768]{1,0:T(8,128)(2,1)} %bitcast.187, bf16[800,768]{1,0:T(8,128)(2,1)S(1)} %bitcast.177, f32[1440,3072]{1,0:T(8,128)} %get-tuple-element.109, ...), kind=kOutput, calls=%fused_computation.4 | convolution fusion | flops 6874395648 | bytes 51191808 | tf_op jit(solution)/shard_map/tj,ij->ti/dot_general | solution.py:182
  397.5 13.7 %multiply_reduce_fusion.1 = (f32[768]{0:T(1024)}, f32[1440]{0:T(1024)S(1)}, f32[768]{0:T(1024)}, f32[1440,768]{1,0:T(8,128)S(1)}) fusion(f32[1440,768]{1,0:T(8,128)S(1)} %get-tuple-element.108, f32[1440]{0:T(1024)S(1)} %fusion.104, f32[1440]{0:T(1024)S(1)} %broadcast_multiply_fusion, f32[768]{0:T(1024)S(1)} %reshape.380, ...), kind=kOutput, calls=%fused_computation.67 | convolution fusion | flops 6803616768 | bytes 22439808 | tf_op jit(solution)/shard_map/tj,ij->ti/dot_general | solution.py:187
  434.4 10.0 %convert_bitcast_fusion.2 = bf16[16,40,1,12,64]{4,1,3,0,2:T(8,128)(2,1)} fusion(f32[16,12,40,40]{2,3,1,0:T(8,128)} %fusion.100, f32[16,12,40,40]{2,3,1,0:T(8,128)} %copy-done.8, f32[16,12,40]{2,1,0:T(8,128)S(1)} %copy-done.35, bf16[16,40,1,12,64]{4,3,2,1,0:T(8,128)(2,1)} %copy-done.26), kind=kOutput, calls=%fused_computation.98 | convolution fusion | flops 41971240 | bytes 4454400 | tf_op jit(solution)/shard_map/chqk,ckhd->cqhd/dot_general | solution.py:59
  475.4 19.7 %fusion.92 = bf16[4,200,1,12,64]{1,4,3,0,2:T(8,128)(2,1)} fusion(f32[4,12,200,200]{2,3,1,0:T(8,128)} %fusion.81, f32[4,12,200]{2,1,0:T(8,128)S(1)} %copy-done.46, f32[4,12,200,200]{2,3,1,0:T(8,128)} %copy-done.3, pred[4,200]{1,0:T(4,128)(4,1)S(1)} %copy-done.52, bf16[4,200,1,12,64]{1,4,3,0,2:T(8,128)(2,1)S(1)} %copy-done.17), kind=kOutput, calls=%fused_computation.122 | convolution fusion | flops 267504192 | bytes 17856800 | tf_op jit(solution)/shard_map/chqk,ckhd->cqhd/dot_general | solution.py:59
  495.1 19.0 %fusion.87 = bf16[4,200,1,12,64]{1,4,3,0,2:T(8,128)(2,1)} fusion(f32[4,12,200,200]{2,3,1,0:T(8,128)} %fusion.81, f32[4,12,200]{2,1,0:T(8,128)S(1)} %copy-done.46, f32[4,12,200,200]{2,3,1,0:T(8,128)} %copy-done.3, pred[4,200]{1,0:T(4,128)(4,1)S(1)} %copy-done.52, bf16[4,200,1,12,64]{1,4,3,0,2:T(8,128)(2,1)S(1)} %copy-done.15), kind=kOutput, calls=%fused_computation.121 | convolution fusion | flops 267504192 | bytes 17856800 | tf_op jit(solution)/shard_map/chqk,cqhd->ckhd/dot_general | solution.py:62
  528.5 12.8 %copy.203 = bf16[16,40,3,12,64]{1,0,4,3,2:T(8,128)(2,1)} copy(bf16[16,40,3,12,64]{4,1,3,0,2:T(8,128)(2,1)} %pad_maximum_fusion.2) | data formatting | bytes 5898240 | tf_op jit(solution)/shard_map/convert_element_type | solution.py:69
  541.2 14.1 %reshape.397 = bf16[640,2304]{0,1:T(8,128)(2,1)} reshape(bf16[16,40,3,12,64]{1,0,4,3,2:T(8,128)(2,1)} %copy.203) | data formatting | bytes 5898240 | tf_op jit(solution)/shard_map/convert_element_type | solution.py:69
  574.4 12.5 %convolution_convert_fusion = bf16[768,2304]{1,0:T(8,128)(2,1)} fusion(bf16[640,2304]{0,1:T(8,128)(2,1)} %reshape.397, bf16[800,2304]{0,1:T(8,128)(2,1)} %convert_element_type.280, f32[768]{0:T(1024)S(1)} %copy-done.54, f32[768]{0:T(1024)S(1)} %copy-done.48, f32[1440]{0:T(1024)S(1)} %copy-done.39, f32[1440]{0:T(1024)S(1)} %copy-done.37, ...), kind=kOutput, calls=%fused_computation.48 | convolution fusion | flops 5121073152 | bytes 12403968 | tf_op jit(solution)/shard_map/ti,tj->ij/dot_general | solution.py:203
  614.7 12.5 %convolution_convert_fusion.1 = bf16[3072,768]{1,0:T(8,128)(2,1)} fusion(bf16[1440,3072]{1,0:T(8,128)(2,1)} %get-tuple-element.75, bf16[640,768]{1,0:T(8,128)(2,1)} %bitcast.188, bf16[800,768]{1,0:T(8,128)(2,1)S(1)} %bitcast.179), kind=kOutput, calls=%fused_computation.49 | convolution fusion | flops 6801555456 | bytes 15777792 | tf_op jit(solution)/shard_map/ti,tj->ij/dot_general | solution.py:180
  639.5 14.0 %convolution_convert_fusion.2 = bf16[768,3072]{1,0:T(8,128)(2,1)} fusion(bf16[1440,3072]{1,0:T(8,128)(2,1)} %get-tuple-element.113, f32[1440,768]{1,0:T(8,128)} %copy-done.6, f32[768]{0:T(1024)S(1)} %copy-done.56, f32[768]{0:T(1024)S(1)} %reshape.380, f32[1440]{0:T(1024)S(1)} %fusion.104, f32[1440]{0:T(1024)S(1)} %broadcast_multiply_fusion), kind=kOutput, calls=%fused_computation.50 | convolution fusion | flops 6802661376 | bytes 18007296 | tf_op jit(solution)/shard_map/ti,tj->ij/dot_general | solution.py:185
  687.3 12.0 %reshape.376 = bf16[32,576,128]{2,1,0:T(8,128)(2,1)} reshape(bf16[8,4,384,192]{3,2,1,0:T(8,128)(2,1)} %copy.194) | data formatting | bytes 9437184 | tf_op jit(solution)/shard_map/reshape | solution.py:96
  708.2 13.1 %add_convert_fusion.2 = bf16[1440,768]{1,0:T(8,128)(2,1)S(1)} fusion(f32[1440,768]{1,0:T(8,128)} %copy-done.6, bf16[1440,3072]{1,0:T(8,128)(2,1)} %get-tuple-element.75, bf16[3072,768]{0,1:T(8,128)(2,1)} %bitcast.181, f32[768]{0:T(1024)S(1)} %reshape.383), kind=kOutput, calls=%fused_computation.71 | convolution fusion | flops 6798090240 | bytes 20204544 | tf_op jit(solution)/shard_map/dot_general | solution.py:176
  723.4 11.4 %fusion.131 = (f32[768]{0:T(1024)S(1)}, f32[1440]{0:T(1024)S(1)}, f32[1440,768]{1,0:T(8,128)S(1)}) fusion(f32[768]{0:T(1024)S(1)} %copy-done.48, f32[1440]{0:T(1024)S(1)} %copy-done.37, bf16[640,768]{1,0:T(8,128)(2,1)S(1)} %bitcast.172, bf16[800,768]{1,0:T(8,128)(2,1)S(1)} %bitcast.156, bf16[768,2304]{1,0:T(8,128)(2,1)} %reshape.351, ...), kind=kOutput, calls=%fused_computation.185 | convolution fusion | flops 5119301120 | bytes 16827648 | tf_op jit(solution)/shard_map/tj,ij->ti/dot_general | solution.py:210
  749.5 18.0 %psum.14 = f32[9216]{0:T(1024)S(1)} all-reduce(f32[9216]{0:T(1024)S(1)} %constant_dynamic-update-slice_fusion), channel_id=1, replica_groups=mesh['img'=8,'seq'=4] {'seq'}, use_global_device_ids=true, to_apply=%region_22.23 | all-reduce | flops 9216 | bytes 73728 | tf_op jit(solution)/shard_map/psum | solution.py:225
  767.4 23.9 %psum.15 = f32[9216]{0:T(1024)S(1)} all-reduce(f32[9216]{0:T(1024)S(1)} %psum.14), channel_id=1, replica_groups=mesh['img'=8,'seq'=4] {'img'}, use_global_device_ids=true, to_apply=%region_23.24 | all-reduce | flops 9216 | bytes 73728 | tf_op jit(solution)/shard_map/psum | solution.py:225
  796.5 64.2 %reduce-scatter.5.cloned.1.call-done = bf16[1,1152,128]{2,1,0:T(8,128)(2,1)} async-done(((bf16[32,1152,128]{2,1,0:T(8,128)(2,1)}), bf16[1,1152,128]{2,1,0:T(8,128)(2,1)}) %reduce-scatter.5.cloned.1.call-update) | async-done | bytes 294928 | tf_op jit(solution)/shard_map/reduce_scatter | solution.py:98
  (302 shorter events, 383.3 us)
Async XLA Ops:
  7.2 15.2 %copy-start = (s32[64,40]{0,1:T(8,128)S(1)}, s32[64,40]{0,1:T(8,128)}, u32[]{:S(2)}) copy-start(s32[64,40]{0,1:T(8,128)} %param.21) | copy-start | bytes 30724
  7.2 15.3 %copy-start.10 = (bf16[16,40,768]{2,1,0:T(8,128)(2,1)S(1)}, bf16[16,40,768]{2,1,0:T(8,128)(2,1)}, u32[]{:S(2)}) copy-start(bf16[16,40,768]{2,1,0:T(8,128)(2,1)} %param.19) | copy-start | bytes 2949124
  7.2 15.3 %copy-start.4 = (bf16[4,200,768]{2,1,0:T(8,128)(2,1)S(1)}, bf16[4,200,768]{2,1,0:T(8,128)(2,1)}, u32[]{:S(2)}) copy-start(bf16[4,200,768]{2,1,0:T(8,128)(2,1)} %param.18) | copy-start | bytes 3686404
  7.2 73.8 %all-gather.7.cloned.1.call-start = ((), (), s32[]{:S(2)}) async-start(), calls=%async_computation.4 | async-start | bytes 4325376 | tf_op jit(solution)/shard_map/all_gather | solution.py:76
  16.0 205.5 %all-gather.9.cloned.1.call-start = ((), (), s32[]{:S(2)}) async-start(), calls=%async_computation.5 | async-start | bytes 11354112 | tf_op jit(solution)/shard_map/all_gather | solution.py:76
  22.3 771.0 %reduce-scatter.3.cloned.1.call-start = ((), (), s32[]{:S(2)}) async-start(), calls=%async_computation.2 | async-start | bytes 4866048 | tf_op jit(solution)/shard_map/reduce_scatter | solution.py:98
  23.6 185.5 %copy-start.51 = (pred[4,200]{1,0:T(4,128)(4,1)}, pred[4,200]{1,0:T(4,128)(4,1)S(1)}, u32[]{:S(2)}) copy-start(pred[4,200]{1,0:T(4,128)(4,1)S(1)} %dynamic-slice_compare_fusion) | copy-start | bytes 2404
  23.6 98.3 %copy-start.36 = (f32[1440]{0:T(1024)}, f32[1440]{0:T(1024)S(1)}, u32[]{:S(2)}) copy-start(f32[1440]{0:T(1024)S(1)} %broadcast_multiply_fusion.1) | copy-start | bytes 17284
  25.0 96.9 %copy-start.38 = (f32[1440]{0:T(1024)}, f32[1440]{0:T(1024)S(1)}, u32[]{:S(2)}) copy-start(f32[1440]{0:T(1024)S(1)} %fusion.103) | copy-start | bytes 17284
  84.5 37.5 %copy-start.53 = (f32[768]{0:T(1024)}, f32[768]{0:T(1024)S(1)}, u32[]{:S(2)}) copy-start(f32[768]{0:T(1024)S(1)} %reshape.378) | copy-start | bytes 9220
  84.7 37.3 %copy-start.47 = (f32[768]{0:T(1024)}, f32[768]{0:T(1024)S(1)}, u32[]{:S(2)}) copy-start(f32[768]{0:T(1024)S(1)} %reshape.377) | copy-start | bytes 9220
  136.4 191.6 %copy-start.55 = (f32[768]{0:T(1024)}, f32[768]{0:T(1024)S(1)}, u32[]{:S(2)}) copy-start(f32[768]{0:T(1024)S(1)} %reshape.381) | copy-start | bytes 9220
  324.5 51.7 %slice-start.2 = ((s8[4718592]{0:T(1024)(128)(4,1)}), s8[524288]{0:T(1024)(128)(4,1)S(1)}, s32[]{:S(2)}) async-start(s8[4718592]{0:T(1024)(128)(4,1)} %bitcast.182), calls=%async_computation.8 | async-start | bytes 1048576
  327.3 83.9 %copy-start.6 = (f32[1440,768]{1,0:T(8,128)}, f32[1440,768]{1,0:T(8,128)S(1)}, u32[]{:S(2)}) copy-start(f32[1440,768]{1,0:T(8,128)S(1)} %get-tuple-element.108) | copy-start | bytes 13271044
  328.0 48.2 %copy-start.44 = (f32[1440]{0:T(1024)}, f32[1440]{0:T(1024)S(1)}, u32[]{:S(2)}) copy-start(f32[1440]{0:T(1024)S(1)} %multiply_reduce_fusion.3) | copy-start | bytes 17284
  328.0 48.2 %copy-start.19 = (bf16[4,200,768]{2,1,0:T(8,128)(2,1)S(1)}, bf16[4,200,768]{2,1,0:T(8,128)(2,1)}, u32[]{:S(2)}) copy-start(bf16[4,200,768]{2,1,0:T(8,128)(2,1)} %param.34) | copy-start | bytes 3686404
  328.0 48.1 %slice-start.3 = ((s8[4718592]{0:T(1024)(128)(4,1)}), s8[4194304]{0:T(1024)(128)(4,1)S(1)}, s32[]{:S(2)}) async-start(s8[4718592]{0:T(1024)(128)(4,1)} %bitcast.182), calls=%async_computation.9 | async-start | bytes 8388608
  475.4 19.7 %copy-start.15 = (bf16[4,200,1,12,64]{1,4,3,0,2:T(8,128)(2,1)S(1)}, bf16[4,200,1,12,64]{1,4,3,0,2:T(8,128)(2,1)}, u32[]{:S(2)}) copy-start(bf16[4,200,1,12,64]{1,4,3,0,2:T(8,128)(2,1)} %copy.213) | copy-start | bytes 3686404
  495.1 19.0 %copy-start.32 = (bf16[768,768]{1,0:T(8,128)(2,1)S(1)}, bf16[768,768]{1,0:T(8,128)(2,1)}, u32[]{:S(2)}) copy-start(bf16[768,768]{1,0:T(8,128)(2,1)} %convolution_convert_fusion.4) | copy-start | bytes 3538948
  613.4 247.3 %reduce-scatter.5.cloned.1.call-start = ((), (), s32[]{:S(2)}) async-start(), calls=%async_computation.3 | async-start | bytes 9732096 | tf_op jit(solution)/shard_map/reduce_scatter | solution.py:98
  708.2 15.2 %copy-start.7 = (bf16[800,2304]{0,1:T(8,128)(2,1)S(1)}, bf16[800,2304]{0,1:T(8,128)(2,1)}, u32[]{:S(2)}) copy-start(bf16[800,2304]{0,1:T(8,128)(2,1)} %convert_element_type.280) | copy-start | bytes 11059204
  722.3 16.6 %slice-start = ((s8[4423680]{0:T(1024)(128)(4,1)}), s8[4194304]{0:T(1024)(128)(4,1)S(1)}, s32[]{:S(2)}) async-start(s8[4423680]{0:T(1024)(128)(4,1)} %bitcast.148), calls=%async_computation.6 | async-start | bytes 8388608
  723.4 15.5 %slice-start.1 = ((s8[4423680]{0:T(1024)(128)(4,1)}), s8[229376]{0:T(1024)(128)(4,1)S(1)}, s32[]{:S(2)}) async-start(s8[4423680]{0:T(1024)(128)(4,1)} %bitcast.148), calls=%async_computation.7 | async-start | bytes 458752
  745.1 118.4 %copy-start.1 = (s32[64,40]{0,1:T(8,128)S(1)}, s32[64,40]{0,1:T(8,128)}, u32[]{:S(2)}) copy-start(s32[64,40]{0,1:T(8,128)} %param.21) | copy-start | bytes 30724
  (43 other events, 238.0 us)
Sparse Core Ops, SparseCore 0:
  16.2 64.7 all-gather.6
  84.4 87.4 all-gather.8
  613.5 105.6 reduce-scatter.2
  726.0 134.6 reduce-scatter.4
